TPU v7x, 32 devices: a whole 2x2x4 slice. The times are simulated.
32 devices in a mesh: blk: 16 (over z, y, core), grp: 2 (over x).
Axes of the slice: x: 2, y: 2, z: 4, core: 2. Of those that a mesh axis runs over, the one named last changes fastest.
Arguments:
- images: float32 [4096, 768], P(('blk', 'grp')), may hold values from -0.24 to 0.24
- texts: float32 [4096, 768], P(('blk', 'grp')), may hold values from -0.24 to 0.24
- log_temp: float32 [1], replicated, may hold values from 2.3 to 3
- bias: float32 [1], replicated, may hold values from -3 to -1
- row_weight: float32 [4096], P(('blk', 'grp')), may hold values from 0.5 to 2
Outputs:
- row_loss: float32 [4096], P(('blk', 'grp'))
- grad_images: float32 [4096, 768], P(('blk', 'grp'))
- grad_texts: float32 [4096, 768], P(('blk', 'grp'))
All inputs are finite; a program needn't handle non-finite values.
Results may differ from a plain program's by a relative error of at most 0.00013.
Values sent between devices are 32-bit elements; how exact they have to be, the bound alone decides.
No kernel may reach another device: no remote copies, remote signals or barrier semaphores. Data moves between devices by JAX's collectives and lax.ppermute only.
A program may use at most 64 MiB of HBM per device.

v0:
```python
import jax
import jax.numpy as jnp
from jax import lax
from jax.sharding import PartitionSpec as P

REACH = 1


def passed_along(x, axis, by):
    length = lax.axis_size(axis)
    return lax.ppermute(x, axis, [(i, (i + by) % length) for i in range(length)])


def normed(values):
    scale = lax.rsqrt(jnp.sum(values * values, axis=1, keepdims=True) + 1e-06)
    return (values * scale, scale)


def unnormed(grad, unit, scale):
    return scale * (grad - unit * jnp.sum(unit * grad, axis=1, keepdims=True))


def tile_terms(left, right, temper, offset_b, weight, positive):
    logits = (
        temper * jnp.einsum("id,jd->ij", left, right, precision=lax.Precision.HIGHEST) + offset_b
    )
    labels = jnp.where(positive, 1.0, -1.0)
    losses = jax.nn.softplus(-labels * logits)
    slope = -labels * jax.nn.sigmoid(-labels * logits) * weight[:, None]
    return (jnp.sum(losses, axis=1), slope)


def shards(images, texts, log_temp, bias, row_weight):
    unit_x, scale_x = normed(images)
    unit_y, scale_y = normed(texts)
    temper = jnp.exp(log_temp[0])
    offset_b = bias[0]
    count = images.shape[0]
    members = lax.axis_size("grp")
    group = count * members
    mine = lax.axis_index("grp")
    group_x, group_w = (
        lax.all_gather(unit_x, "grp", axis=0, tiled=True),
        lax.all_gather(row_weight, "grp", axis=0, tiled=True),
    )
    window = {0: unit_y}
    current = unit_y
    step = 1
    current = passed_along(current, "blk", -1)
    window[step] = current
    current = unit_y
    step = 1
    current = passed_along(current, "blk", 1)
    window[-step] = current
    rows = lax.broadcasted_iota(jnp.int32, (group, count), 0)
    cols = lax.broadcasted_iota(jnp.int32, (group, count), 1)
    diagonal = rows == mine * count + cols
    nothing = jnp.zeros((group, count), bool)
    grad_group = jnp.zeros_like(group_x)
    group_sums = jnp.zeros((group,), jnp.float32)
    text_terms = {}
    for offset in range(-REACH, REACH + 1):
        positive = diagonal if offset == 0 else nothing
        part_sums, slope = tile_terms(group_x, window[offset], temper, offset_b, group_w, positive)
        group_sums = group_sums + part_sums
        grad_group = grad_group + temper * jnp.dot(
            slope, window[offset], precision=lax.Precision.HIGHEST
        )
        text_terms[offset] = temper * jnp.einsum(
            "ij,id->jd", slope, group_x, precision=lax.Precision.HIGHEST
        )
    step = 1
    carried = passed_along(text_terms[step], "blk", 1)
    step = 1
    returned = passed_along(text_terms[-step], "blk", -1)
    grad_y = text_terms[0] + carried + returned
    grad_x, sums = (
        lax.psum_scatter(grad_group, "grp", scatter_dimension=0, tiled=True),
        lax.psum_scatter(group_sums, "grp", scatter_dimension=0, tiled=True),
    )
    row_loss = sums / ((2 * REACH + 1) * group)
    return (row_loss, unnormed(grad_x, unit_x, scale_x), unnormed(grad_y, unit_y, scale_y))


def solution(mesh):
    placed = (P(("blk", "grp"), None), P(("blk", "grp"), None), P(), P(), P(("blk", "grp")))
    return jax.shard_map(
        shards,
        mesh=mesh,
        in_specs=placed,
        out_specs=(P(("blk", "grp")), P(("blk", "grp"), None), P(("blk", "grp"), None)),
        check_vma=False,
    )
```

profile of v0, /device:TPU:0, one launch (start us, length us, event | category | flops | bytes accessed | tf_op | source)
XLA Modules:
  0.0 63.5 jit_solution(8459419432554972889)
XLA Ops:
  7.2 0.0 copy-start.1
  7.2 0.0 reduce-scatter.2.cloned.1.call-start
  7.2 1.1 %multiply_reduce_fusion.2 = f32[128]{0:T(128)S(1)} fusion(f32[128,768]{1,0:T(8,128)} %param.6), kind=kLoop, calls=%fused_computation.19 | loop fusion | flops 196480 | bytes 393728 | tf_op jit(solution)/shard_map/reduce_sum | solution.py:15
  8.4 0.0 copy-done.1
  8.4 0.0 copy-start
  8.4 0.1 broadcast_multiply_fusion
  8.5 5.5 %collective-permute-start.1 = (f32[128,768]{1,0:T(8,128)S(1)}, f32[128,768]{1,0:T(8,128)S(1)}, u32[]{:S(2)}, u32[]{:S(2)}) collective-permute-start(f32[128,768]{1,0:T(8,128)S(1)} %broadcast_multiply_fusion), channel_id=1, source_target_pairs={{0,30},{2,0},{4,2},{6,4},{8,6},{10,8},{12,10},{14,12},{16,14},{18,... | collective-permute-start | bytes 1179656 | tf_op jit(solution)/shard_map/ppermute | solution.py:11
  14.0 0.0 collective-permute-start
  14.7 0.0 copy-done
  14.7 0.1 multiply_reduce_fusion.3
  14.8 0.1 broadcast_multiply_fusion.1
  14.9 9.4 %all_gather.6 = f32[256,768]{1,0:T(8,128)S(1)} all-gather(f32[128,768]{1,0:T(8,128)S(1)} %broadcast_multiply_fusion.1), channel_id=1, replica_groups=mesh['blk'=16,'grp'=2] {'grp'}, dimensions={0}, use_global_device_ids=true | all-gather | bytes 1179648 | tf_op jit(solution)/shard_map/all_gather | solution.py:43
  25.0 0.0 copy-start.3
  25.0 0.6 %copy-done.3 = f32[128]{0:T(128)S(1)} copy-done((f32[128]{0:T(128)S(1)}, f32[128]{0:T(128)}, u32[]{:S(2)}) %copy-start.3) | copy-done | bytes 536
  25.7 4.2 %all-gather = f32[2,1,128]{2,1,0:T(1,128)S(1)} all-gather(f32[1,1,128]{2,1,0:T(1,128)S(1)} %bitcast.26), channel_id=1, replica_groups=mesh['blk'=16,'grp'=2] {'grp'}, dimensions={0}, use_global_device_ids=true | all-gather | bytes 1536 | tf_op jit(solution)/shard_map/all_gather | solution.py:44
  29.9 1.0 %fusion.9 = (f32[256]{0:T(256)S(1)}, f32[256,128]{0,1:T(8,128)S(1)}) fusion(f32[]{:T(128)} %bitcast.19, f32[256,768]{1,0:T(8,128)S(1)} %all_gather.6, f32[128,768]{1,0:T(8,128)S(1)} %broadcast_multiply_fusion, f32[]{:T(128)} %bitcast, s32[128]{0:T(128)S(1)} %iota_add_fusion), kind=kOutput, calls=%fused_computation.27 | convolution fusion | flops 302415616 | bytes 1312264 | tf_op jit(solution)/shard_map/id,jd->ij/dot_general | solution.py:25
  30.9 0.9 %fusion.16 = f32[256,768]{1,0:T(8,128)S(1)} fusion(f32[128,768]{1,0:T(8,128)S(1)} %broadcast_multiply_fusion, f32[256,128]{0,1:T(8,128)S(1)} %get-tuple-element.8, f32[256]{0:T(256)S(1)} %bitcast.20, s32[128]{0:T(128)S(1)} %iota_add_fusion), kind=kOutput, calls=%fused_computation.44 | convolution fusion | flops 302252032 | bytes 1312256 | tf_op jit(solution)/shard_map/dot_general | solution.py:66
  31.8 0.0 collective-permute-done.1
  31.8 1.0 %fusion.10 = (f32[256]{0:T(256)S(1)}, f32[256,128]{0,1:T(8,128)S(1)}) fusion(f32[]{:T(128)} %bitcast.18, f32[256,768]{1,0:T(8,128)S(1)} %all_gather.6, f32[128,768]{1,0:T(8,128)S(1)} %collective-permute-done.1, f32[]{:T(128)} %bitcast), kind=kOutput, calls=%fused_computation.28 | convolution fusion | flops 302284544 | bytes 1311752 | tf_op jit(solution)/shard_map/id,jd->ij/dot_general | solution.py:25
  32.8 0.8 %fusion.11 = f32[256,768]{1,0:T(8,128)S(1)} fusion(f32[128,768]{1,0:T(8,128)S(1)} %collective-permute-done.1, f32[256,128]{0,1:T(8,128)S(1)} %get-tuple-element.4, f32[256]{0:T(256)S(1)} %bitcast.21), kind=kOutput, calls=%fused_computation.34 | convolution fusion | flops 302120960 | bytes 1311744 | tf_op jit(solution)/shard_map/dot_general | solution.py:66
  33.7 0.0 collective-permute-done
  33.7 1.0 %fusion.8 = (f32[256]{0:T(256)S(1)}, f32[256,128]{0,1:T(8,128)S(1)}) fusion(f32[]{:T(128)} %bitcast.17, f32[256,768]{1,0:T(8,128)S(1)} %all_gather.6, f32[128,768]{1,0:T(8,128)S(1)} %collective-permute-done, f32[]{:T(128)} %bitcast), kind=kOutput, calls=%fused_computation.26 | convolution fusion | flops 302284544 | bytes 1311752 | tf_op jit(solution)/shard_map/id,jd->ij/dot_general | solution.py:25
  34.7 1.7 %fusion.1 = f32[256,768]{1,0:T(8,128)} fusion(f32[256,768]{1,0:T(8,128)S(1)} %fusion.11, f32[256,768]{1,0:T(8,128)S(1)} %fusion.16, f32[128,768]{1,0:T(8,128)S(1)} %collective-permute-done, f32[]{:T(128)} %bitcast, f32[256,128]{0,1:T(8,128)S(1)} %get-tuple-element.6, f32[256]{0:T(256)S(1)} %bitcast.22), kind=kOutput, calls=%fused_computation.2 | convolution fusion | flops 302710784 | bytes 2884612 | tf_op jit(solution)/shard_map/dot_general | solution.py:66
  36.4 0.0 reduce-scatter.2.cloned.1.call-update
  36.4 1.3 %convolution_multiply_fusion = f32[128,768]{1,0:T(8,128)} fusion(f32[256,768]{1,0:T(8,128)S(1)} %all_gather.6, f32[]{:T(128)} %bitcast, f32[256,128]{0,1:T(8,128)S(1)} %get-tuple-element.6, f32[256]{0:T(256)S(1)} %bitcast.23), kind=kOutput, calls=%fused_computation.3 | convolution fusion | flops 302219264 | bytes 1311748 | tf_op jit(solution)/shard_map/ij,id->jd/dot_general | solution.py:69
  37.8 0.6 convolution_multiply_fusion.1
  38.4 2.7 %collective-permute-start.3 = (f32[128,768]{1,0:T(8,128)}, f32[128,768]{1,0:T(8,128)S(1)}, u32[]{:S(2)}, u32[]{:S(2)}) collective-permute-start(f32[128,768]{1,0:T(8,128)} %convolution_multiply_fusion), channel_id=1, source_target_pairs={{0,30},{2,0},{4,2},{6,4},{8,6},{10,8},{12,10},{14,12},{16,14},{18,... | collective-permute-start | bytes 1179656 | tf_op jit(solution)/shard_map/ppermute | solution.py:11
  41.0 0.0 collective-permute-start.2
  41.0 0.0 copy-start.4
  41.0 0.7 %copy-done.4 = u32[32]{0:T(128)S(1)} copy-done((u32[32]{0:T(128)S(1)}, u32[32]{0:T(128)}, u32[]{:S(2)}) %copy-start.4) | copy-done | bytes 152
  41.7 0.6 dynamic-slice
  42.9 5.1 %all-reduce = f32[256]{0:T(256)S(1)} all-reduce(f32[256]{0:T(256)S(1)} %add_add_fusion), channel_id=2, replica_groups=mesh['blk'=16,'grp'=2] {'grp'}, use_global_device_ids=true, to_apply=%region_5.6.clone | all-reduce | flops 256 | bytes 2048
  48.1 0.6 dynamic-slice_multiply_fusion
  48.7 0.0 collective-permute-done.3
  48.7 2.3 %collective-permute-done.2 = f32[128,768]{1,0:T(8,128)S(1)} collective-permute-done((f32[128,768]{1,0:T(8,128)S(1)}, f32[128,768]{1,0:T(8,128)S(1)}, u32[]{:S(2)}, u32[]{:S(2)}) %collective-permute-start.2) | collective-permute-done | bytes 393248 | tf_op jit(solution)/shard_map/ppermute | solution.py:11
  50.9 0.7 %multiply_reduce_fusion = (f32[128]{0:T(128)S(1)}, f32[128,768]{1,0:T(8,128)S(1)}) fusion(f32[128,768]{1,0:T(8,128)S(1)} %broadcast_multiply_fusion, f32[128,768]{1,0:T(8,128)S(1)} %collective-permute-done.3, f32[128,768]{1,0:T(8,128)S(1)} %collective-permute-done.2, f32[256,768]{1,0:T(8,128)S(1)} %all_gather.6, f32[256,128]{0,1:T(8,128)S(1)} %get-tuple-element.8, ...), kind=kOutput, calls=%fused_computation.16 | convolution fusion | flops 302743424 | bytes 2492420 | tf_op jit(solution)/shard_map/ij,id->jd/dot_general | solution.py:69
  51.6 0.9 %subtract_multiply_fusion = f32[128,768]{1,0:T(8,128)} fusion(f32[128,768]{1,0:T(8,128)S(1)} %get-tuple-element.10, f32[128]{0:T(128)S(1)} %get-tuple-element.9, f32[128]{0:T(128)S(1)} %add_rsqrt_fusion, f32[128,768]{1,0:T(8,128)S(1)} %copy-done.1), kind=kLoop, calls=%fused_computation.15 | loop fusion | flops 393216 | bytes 1180672 | tf_op jit(solution)/shard_map/mul | solution.py:20
  52.5 1.9 %reduce-scatter.2.cloned.1.call-done = f32[128,768]{1,0:T(8,128)} async-done(((f32[256,768]{1,0:T(8,128)}), f32[128,768]{1,0:T(8,128)}) %reduce-scatter.2.cloned.1.call-update) | async-done | bytes 393232 | tf_op jit(solution)/shard_map/reduce_scatter | solution.py:78
  54.5 0.0 copy-start.2
  54.5 1.2 %multiply_reduce_fusion.1 = f32[128]{0:T(128)S(1)} fusion(f32[128,768]{1,0:T(8,128)} %reduce-scatter.2.cloned.1.call-done, f32[128,768]{1,0:T(8,128)S(1)} %copy-done, f32[128]{0:T(128)S(1)} %add_rsqrt_fusion.1), kind=kLoop, calls=%fused_computation.18 | loop fusion | flops 294784 | bytes 787456 | tf_op jit(solution)/shard_map/reduce_sum | solution.py:20
  55.7 0.0 copy-done.2
  55.7 0.9 %subtract_multiply_fusion.1 = f32[128,768]{1,0:T(8,128)} fusion(f32[128,768]{1,0:T(8,128)S(1)} %copy-done.2, f32[128]{0:T(128)S(1)} %multiply_reduce_fusion.1, f32[128]{0:T(128)S(1)} %add_rsqrt_fusion.1, f32[128,768]{1,0:T(8,128)S(1)} %copy-done), kind=kLoop, calls=%fused_computation.17 | loop fusion | flops 393216 | bytes 1180672 | tf_op jit(solution)/shard_map/mul | solution.py:20
  (4 shorter events, 0.0 us)
Async XLA Ops:
  7.2 1.2 %copy-start.1 = (f32[128,768]{1,0:T(8,128)S(1)}, f32[128,768]{1,0:T(8,128)}, u32[]{:S(2)}) copy-start(f32[128,768]{1,0:T(8,128)} %param.6) | copy-start | bytes 1179652
  7.2 47.3 %reduce-scatter.2.cloned.1.call-start = ((), (), s32[]{:S(2)}) async-start(), calls=%async_computation.1 | async-start | bytes 1179648 | tf_op jit(solution)/shard_map/reduce_scatter | solution.py:78
  8.4 6.3 %copy-start = (f32[128,768]{1,0:T(8,128)S(1)}, f32[128,768]{1,0:T(8,128)}, u32[]{:S(2)}) copy-start(f32[128,768]{1,0:T(8,128)} %param.5) | copy-start | bytes 1179652
  8.5 23.3 %collective-permute-start.1 = (f32[128,768]{1,0:T(8,128)S(1)}, f32[128,768]{1,0:T(8,128)S(1)}, u32[]{:S(2)}, u32[]{:S(2)}) collective-permute-start(f32[128,768]{1,0:T(8,128)S(1)} %broadcast_multiply_fusion), channel_id=1, source_target_pairs={{0,30},{2,0},{4,2},{6,4},{8,6},{10,8},{12,10},{14,12},{16,14},{18,... | collective-permute-start | bytes 1179656 | tf_op jit(solution)/shard_map/ppermute | solution.py:11
  14.0 19.6 %collective-permute-start = (f32[128,768]{1,0:T(8,128)S(1)}, f32[128,768]{1,0:T(8,128)S(1)}, u32[]{:S(2)}, u32[]{:S(2)}) collective-permute-start(f32[128,768]{1,0:T(8,128)S(1)} %broadcast_multiply_fusion), channel_id=1, source_target_pairs={{0,2},{2,4},{4,6},{6,8},{8,10},{10,12},{12,14},{14,16},{16,18},{18... | collective-permute-start | bytes 1179656 | tf_op jit(solution)/shard_map/ppermute | solution.py:11
  25.0 0.7 %copy-start.3 = (f32[128]{0:T(128)S(1)}, f32[128]{0:T(128)}, u32[]{:S(2)}) copy-start(f32[128]{0:T(128)} %param.9) | copy-start | bytes 1540
  38.4 10.3 %collective-permute-start.3 = (f32[128,768]{1,0:T(8,128)}, f32[128,768]{1,0:T(8,128)S(1)}, u32[]{:S(2)}, u32[]{:S(2)}) collective-permute-start(f32[128,768]{1,0:T(8,128)} %convolution_multiply_fusion), channel_id=1, source_target_pairs={{0,30},{2,0},{4,2},{6,4},{8,6},{10,8},{12,10},{14,12},{16,14},{18,... | collective-permute-start | bytes 1179656 | tf_op jit(solution)/shard_map/ppermute | solution.py:11
  41.0 9.9 %collective-permute-start.2 = (f32[128,768]{1,0:T(8,128)S(1)}, f32[128,768]{1,0:T(8,128)S(1)}, u32[]{:S(2)}, u32[]{:S(2)}) collective-permute-start(f32[128,768]{1,0:T(8,128)S(1)} %convolution_multiply_fusion.1), channel_id=1, source_target_pairs={{0,2},{2,4},{4,6},{6,8},{8,10},{10,12},{12,14},{14,16},{16,18},{18... | collective-permute-start | bytes 1179656 | tf_op jit(solution)/shard_map/ppermute | solution.py:11
  41.0 0.7 %copy-start.4 = (u32[32]{0:T(128)S(1)}, u32[32]{0:T(128)}, u32[]{:S(2)}) copy-start(u32[32]{0:T(128)} %constant.26) | copy-start | bytes 388
  54.5 1.3 %copy-start.2 = (f32[128,768]{1,0:T(8,128)S(1)}, f32[128,768]{1,0:T(8,128)}, u32[]{:S(2)}) copy-start(f32[128,768]{1,0:T(8,128)} %reduce-scatter.2.cloned.1.call-done) | copy-start | bytes 1179652
Sparse Core Ops, SparseCore 0:
  36.5 17.8 reduce-scatter.1
where the time goes:
time: 63.7 us; the launch traced here: 63.5 us
  blocking collectives  18.7 us (29%)
  between operations  16.2 us (25%)
  matrix products  9.09 us (14%)
  starting transfers between devices  8.24 us (13%)
  other arithmetic  5.08 us (8%)
  waiting for transfers between devices  4.21 us (7%)
  local copies, waits for them, and re-layouts  1.9 us (3%)
    all_gather x1, blocking collectives, shards(): lax.all_gather(unit_x, 'grp', axis=0, tiled=True)  9.38 us
    ppermute x4, starting transfers between devices, passed_along(): lax.ppermute(x, axis, [(i, (i + by) % length) for i in range(length)])  8.2 us
    unnamed x1, blocking collectives  5.14 us
    all_gather x1, blocking collectives, shards(): lax.all_gather(row_weight, 'grp', axis=0, tiled=True)  4.22 us
    dot_general x3, matrix products, shards(): jnp.dot(slope, window[offset], precision=lax.Precision.HIGHEST)  3.45 us
    dot_general x3, matrix products, tile_terms(): jnp.einsum('id,jd->ij', left, right, precision=lax.Precision.HIGHEST)  3 us
    dot_general x3, matrix products, shards(): jnp.einsum('ij,id->jd', slope, group_x, precision=lax.Precision.HIGHEST)  2.65 us
    ppermute x4, waiting for transfers between devices, passed_along(): lax.ppermute(x, axis, [(i, (i + by) % length) for i in range(length)])  2.26 us
  transfers between devices with their start and end apart: 5, of which 2 were waited for; matrix products, arithmetic and copies ran while one was open for 14% of the time, Pallas kernels for 0%

commit v1 on v0

--- a/solution.py
+++ b/solution.py
@@ -4,6 +4,18 @@
 from jax.sharding import PartitionSpec as P
 
 REACH = 1
+
+
+def collect(x, axis, dim):
+    ways, here = (lax.axis_size(axis), lax.axis_index(axis))
+    grown, reach = (x, 1)
+    while reach < ways:
+        theirs = lax.ppermute(grown, axis, [(d, d ^ reach) for d in range(ways)])
+        mine_first = jnp.concatenate([grown, theirs], axis=dim)
+        theirs_first = jnp.concatenate([theirs, grown], axis=dim)
+        grown = jnp.where(here & reach == 0, mine_first, theirs_first)
+        reach = 2 * reach
+    return grown
 
 
 def passed_along(x, axis, by):
@@ -41,7 +53,7 @@
     mine = lax.axis_index("grp")
     group_x, group_w = (
         lax.all_gather(unit_x, "grp", axis=0, tiled=True),
-        lax.all_gather(row_weight, "grp", axis=0, tiled=True),
+        collect(row_weight, "grp", 0),
     )
     window = {0: unit_y}
     current = unit_y

time: 63.7 us -> 59.6 us (0.936)
  blocking collectives: 18.7 us -> 14.3 us
  starting transfers between devices: 8.24 us -> 11.1 us
  waiting for transfers between devices: 4.21 us -> 2.33 us
  local copies, waits for them, and re-layouts: 1.9 us -> 1.26 us
    all_gather x1 -> x0, blocking collectives: 4.22 us -> none  [shards(): lax.all_gather(row_weight, 'grp', axis=0, tiled=True)]
    reduce_scatter x1, waiting for transfers between devices: 1.94 us -> 0.05 us  [shards(): lax.psum_scatter(grad_group, 'grp', scatter_dimension=0, tiled=True)]
    ppermute x0 -> x1, starting transfers between devices: none -> 1.49 us  [collect(): theirs = lax.ppermute(grown, axis, [(d, d ^ reach) for d in range(ways)])]
    ppermute x4, starting transfers between devices: 8.2 us -> 9.62 us  [passed_along(): lax.ppermute(x, axis, [(i, (i + by) % length) for i in range(length)])]
    unnamed x11, local copies, waits for them, and re-layouts: 1.9 us -> 1.26 us
  transfers between devices with their start and end apart: 5 -> 6, of which waited for: 2 -> 1; matrix products, arithmetic and copies ran while one was open for 14% -> 15% of each run, Pallas kernels for 0% -> 0%
where the time goes in v1:
time: 59.6 us; the launch traced here: 59.4 us
  between operations  16.2 us (27%)
  blocking collectives  14.3 us (24%)
  starting transfers between devices  11.1 us (19%)
  matrix products  9.11 us (15%)
  other arithmetic  5.09 us (9%)
  waiting for transfers between devices  2.33 us (4%)
  local copies, waits for them, and re-layouts  1.26 us (2%)
    ppermute x4, starting transfers between devices, passed_along(): lax.ppermute(x, axis, [(i, (i + by) % length) for i in range(length)])  9.62 us
    all_gather x1, blocking collectives, shards(): lax.all_gather(unit_x, 'grp', axis=0, tiled=True)  9.11 us
    unnamed x1, blocking collectives  5.14 us
    dot_general x3, matrix products, shards(): jnp.dot(slope, window[offset], precision=lax.Precision.HIGHEST)  3.46 us
    dot_general x3, matrix products, tile_terms(): jnp.einsum('id,jd->ij', left, right, precision=lax.Precision.HIGHEST)  3 us
    dot_general x3, matrix products, shards(): jnp.einsum('ij,id->jd', slope, group_x, precision=lax.Precision.HIGHEST)  2.65 us
    ppermute x4, waiting for transfers between devices, passed_along(): lax.ppermute(x, axis, [(i, (i + by) % length) for i in range(length)])  2.27 us
    mul x2, other arithmetic, unnormed(): return scale * (grad - unit * jnp.sum(unit * grad, axis=1, keepdims=True))  1.77 us
  transfers between devices with their start and end apart: 6, of which 1 were waited for; matrix products, arithmetic and copies ran while one was open for 15% of the time, Pallas kernels for 0%

profile of v1, /device:TPU:0, one launch (start us, length us, event | category | flops | bytes accessed | tf_op | source)
XLA Modules:
  0.0 59.4 jit_solution(1640335175316993740)
XLA Ops:
  7.2 0.0 copy-start.1
  7.2 0.0 reduce-scatter.2.cloned.1.call-start
  7.2 1.1 %multiply_reduce_fusion.2 = f32[128]{0:T(128)S(1)} fusion(f32[128,768]{1,0:T(8,128)} %param.6), kind=kLoop, calls=%fused_computation.19 | loop fusion | flops 196480 | bytes 393728 | tf_op jit(solution)/shard_map/reduce_sum | solution.py:27
  8.4 0.0 copy-done.1
  8.4 0.0 copy-start.3
  8.4 0.0 copy-start
  8.4 0.1 broadcast_multiply_fusion
  8.5 5.5 %collective-permute-start.1 = (f32[128,768]{1,0:T(8,128)S(1)}, f32[128,768]{1,0:T(8,128)S(1)}, u32[]{:S(2)}, u32[]{:S(2)}) collective-permute-start(f32[128,768]{1,0:T(8,128)S(1)} %broadcast_multiply_fusion), channel_id=1, source_target_pairs={{0,30},{2,0},{4,2},{6,4},{8,6},{10,8},{12,10},{14,12},{16,14},{18,... | collective-permute-start | bytes 1179656 | tf_op jit(solution)/shard_map/ppermute | solution.py:23
  14.0 0.0 collective-permute-start
  14.0 0.0 copy-done.3
  14.0 1.5 %collective-permute-start.2 = (f32[128]{0:T(128)S(1)}, f32[128]{0:T(128)S(1)}, u32[]{:S(2)}, u32[]{:S(2)}) collective-permute-start(f32[128]{0:T(128)S(1)} %copy-done.3), channel_id=1, source_target_pairs={{0,1},{1,0},{2,3},{3,2},{4,5},{5,4},{6,7},{7,6},{8,9},{9,8},{10,11... | collective-permute-start | bytes 1544 | tf_op jit(solution)/shard_map/ppermute | solution.py:13
  16.2 0.0 copy-done
  16.2 0.1 multiply_reduce_fusion.3
  16.3 0.1 broadcast_multiply_fusion.1
  16.4 9.1 %all_gather.3 = f32[256,768]{1,0:T(8,128)S(1)} all-gather(f32[128,768]{1,0:T(8,128)S(1)} %broadcast_multiply_fusion.1), channel_id=1, replica_groups=mesh['blk'=16,'grp'=2] {'grp'}, dimensions={0}, use_global_device_ids=true | all-gather | bytes 1179648 | tf_op jit(solution)/shard_map/all_gather | solution.py:55
  26.3 1.0 %fusion.9 = (f32[256]{0:T(256)S(1)}, f32[256,128]{0,1:T(8,128)S(1)}) fusion(f32[]{:T(128)} %bitcast.17, f32[256,768]{1,0:T(8,128)S(1)} %all_gather.3, f32[128,768]{1,0:T(8,128)S(1)} %broadcast_multiply_fusion, f32[]{:T(128)} %bitcast, s32[128]{0:T(128)S(1)} %iota_add_fusion), kind=kOutput, calls=%fused_computation.27 | convolution fusion | flops 302415616 | bytes 1312264 | tf_op jit(solution)/shard_map/id,jd->ij/dot_general | solution.py:37
  27.3 0.0 collective-permute-done.2
  27.3 0.9 %fusion.16 = f32[256,768]{1,0:T(8,128)S(1)} fusion(f32[128,768]{1,0:T(8,128)S(1)} %broadcast_multiply_fusion, f32[256,128]{0,1:T(8,128)S(1)} %get-tuple-element.8, f32[256]{0:T(256)S(1)} %maximum_select_fusion, s32[128]{0:T(128)S(1)} %iota_add_fusion), kind=kOutput, calls=%fused_computation.45 | convolution fusion | flops 302252032 | bytes 1312256 | tf_op jit(solution)/shard_map/dot_general | solution.py:78
  28.2 0.0 collective-permute-done.1
  28.2 1.0 %fusion.10 = (f32[256]{0:T(256)S(1)}, f32[256,128]{0,1:T(8,128)S(1)}) fusion(f32[]{:T(128)} %bitcast.16, f32[256,768]{1,0:T(8,128)S(1)} %all_gather.3, f32[128,768]{1,0:T(8,128)S(1)} %collective-permute-done.1, f32[]{:T(128)} %bitcast), kind=kOutput, calls=%fused_computation.28 | convolution fusion | flops 302284544 | bytes 1311752 | tf_op jit(solution)/shard_map/id,jd->ij/dot_general | solution.py:37
  29.2 0.8 %fusion.11 = f32[256,768]{1,0:T(8,128)S(1)} fusion(f32[128,768]{1,0:T(8,128)S(1)} %collective-permute-done.1, f32[256,128]{0,1:T(8,128)S(1)} %get-tuple-element.4, f32[256]{0:T(256)S(1)} %maximum_select_fusion), kind=kOutput, calls=%fused_computation.34 | convolution fusion | flops 302120960 | bytes 1311744 | tf_op jit(solution)/shard_map/dot_general | solution.py:78
  30.0 0.0 collective-permute-done
  30.1 1.0 %fusion.8 = (f32[256]{0:T(256)S(1)}, f32[256,128]{0,1:T(8,128)S(1)}) fusion(f32[]{:T(128)} %bitcast.15, f32[256,768]{1,0:T(8,128)S(1)} %all_gather.3, f32[128,768]{1,0:T(8,128)S(1)} %collective-permute-done, f32[]{:T(128)} %bitcast), kind=kOutput, calls=%fused_computation.26 | convolution fusion | flops 302284544 | bytes 1311752 | tf_op jit(solution)/shard_map/id,jd->ij/dot_general | solution.py:37
  31.1 1.7 %fusion.1 = f32[256,768]{1,0:T(8,128)} fusion(f32[256,768]{1,0:T(8,128)S(1)} %fusion.11, f32[256,768]{1,0:T(8,128)S(1)} %fusion.16, f32[128,768]{1,0:T(8,128)S(1)} %collective-permute-done, f32[]{:T(128)} %bitcast, f32[256,128]{0,1:T(8,128)S(1)} %get-tuple-element.6, f32[256]{0:T(256)S(1)} %maximum_select_fusion), kind=kOutput, calls=%fused_computation.2 | convolution fusion | flops 302710784 | bytes 2884612 | tf_op jit(solution)/shard_map/dot_general | solution.py:78
  32.8 0.0 reduce-scatter.2.cloned.1.call-update
  32.8 1.3 %convolution_multiply_fusion = f32[128,768]{1,0:T(8,128)} fusion(f32[256,768]{1,0:T(8,128)S(1)} %all_gather.3, f32[]{:T(128)} %bitcast, f32[256,128]{0,1:T(8,128)S(1)} %get-tuple-element.6, f32[256]{0:T(256)S(1)} %maximum_select_fusion), kind=kOutput, calls=%fused_computation.3 | convolution fusion | flops 302219264 | bytes 1311748 | tf_op jit(solution)/shard_map/ij,id->jd/dot_general | solution.py:81
  34.2 0.6 convolution_multiply_fusion.1
  34.8 4.1 %collective-permute-start.4 = (f32[128,768]{1,0:T(8,128)}, f32[128,768]{1,0:T(8,128)S(1)}, u32[]{:S(2)}, u32[]{:S(2)}) collective-permute-start(f32[128,768]{1,0:T(8,128)} %convolution_multiply_fusion), channel_id=1, source_target_pairs={{0,30},{2,0},{4,2},{6,4},{8,6},{10,8},{12,10},{14,12},{16,14},{18,... | collective-permute-start | bytes 1179656 | tf_op jit(solution)/shard_map/ppermute | solution.py:23
  38.8 0.0 collective-permute-start.3
  38.8 0.0 copy-start.4
  38.8 0.7 %copy-done.4 = u32[32]{0:T(128)S(1)} copy-done((u32[32]{0:T(128)S(1)}, u32[32]{0:T(128)}, u32[]{:S(2)}) %copy-start.4) | copy-done | bytes 152
  39.5 0.6 dynamic-slice
  40.7 5.1 %all-reduce = f32[256]{0:T(256)S(1)} all-reduce(f32[256]{0:T(256)S(1)} %add_add_fusion), channel_id=2, replica_groups=mesh['blk'=16,'grp'=2] {'grp'}, use_global_device_ids=true, to_apply=%region_5.6.clone | all-reduce | flops 256 | bytes 2048
  45.9 0.6 dynamic-slice_multiply_fusion
  46.5 0.0 collective-permute-done.4
  46.5 2.3 %collective-permute-done.3 = f32[128,768]{1,0:T(8,128)S(1)} collective-permute-done((f32[128,768]{1,0:T(8,128)S(1)}, f32[128,768]{1,0:T(8,128)S(1)}, u32[]{:S(2)}, u32[]{:S(2)}) %collective-permute-start.3) | collective-permute-done | bytes 393248 | tf_op jit(solution)/shard_map/ppermute | solution.py:23
  48.7 0.7 %multiply_reduce_fusion = (f32[128]{0:T(128)S(1)}, f32[128,768]{1,0:T(8,128)S(1)}) fusion(f32[128,768]{1,0:T(8,128)S(1)} %broadcast_multiply_fusion, f32[128,768]{1,0:T(8,128)S(1)} %collective-permute-done.4, f32[128,768]{1,0:T(8,128)S(1)} %collective-permute-done.3, f32[256,768]{1,0:T(8,128)S(1)} %all_gather.3, f32[256,128]{0,1:T(8,128)S(1)} %get-tuple-element.8, ...), kind=kOutput, calls=%fused_computation.16 | convolution fusion | flops 302743424 | bytes 2492420 | tf_op jit(solution)/shard_map/ij,id->jd/dot_general | solution.py:81
  49.5 0.9 %subtract_multiply_fusion = f32[128,768]{1,0:T(8,128)} fusion(f32[128,768]{1,0:T(8,128)S(1)} %get-tuple-element.10, f32[128]{0:T(128)S(1)} %get-tuple-element.9, f32[128]{0:T(128)S(1)} %add_rsqrt_fusion, f32[128,768]{1,0:T(8,128)S(1)} %copy-done.1), kind=kLoop, calls=%fused_computation.15 | loop fusion | flops 393216 | bytes 1180672 | tf_op jit(solution)/shard_map/mul | solution.py:32
  50.3 0.0 reduce-scatter.2.cloned.1.call-done
  50.4 0.0 copy-start.2
  50.4 1.2 %multiply_reduce_fusion.1 = f32[128]{0:T(128)S(1)} fusion(f32[128,768]{1,0:T(8,128)} %reduce-scatter.2.cloned.1.call-done, f32[128,768]{1,0:T(8,128)S(1)} %copy-done, f32[128]{0:T(128)S(1)} %add_rsqrt_fusion.1), kind=kLoop, calls=%fused_computation.18 | loop fusion | flops 294784 | bytes 787456 | tf_op jit(solution)/shard_map/reduce_sum | solution.py:32
  51.6 0.0 copy-done.2
  51.7 0.9 %subtract_multiply_fusion.1 = f32[128,768]{1,0:T(8,128)} fusion(f32[128,768]{1,0:T(8,128)S(1)} %copy-done.2, f32[128]{0:T(128)S(1)} %multiply_reduce_fusion.1, f32[128]{0:T(128)S(1)} %add_rsqrt_fusion.1, f32[128,768]{1,0:T(8,128)S(1)} %copy-done), kind=kLoop, calls=%fused_computation.17 | loop fusion | flops 393216 | bytes 1180672 | tf_op jit(solution)/shard_map/mul | solution.py:32
  (5 shorter events, 0.0 us)
Async XLA Ops:
  7.2 1.2 %copy-start.1 = (f32[128,768]{1,0:T(8,128)S(1)}, f32[128,768]{1,0:T(8,128)}, u32[]{:S(2)}) copy-start(f32[128,768]{1,0:T(8,128)} %param.6) | copy-start | bytes 1179652
  7.2 43.2 %reduce-scatter.2.cloned.1.call-start = ((), (), s32[]{:S(2)}) async-start(), calls=%async_computation.1 | async-start | bytes 1179648 | tf_op jit(solution)/shard_map/reduce_scatter | solution.py:90
  8.4 5.7 %copy-start.3 = (f32[128]{0:T(128)S(1)}, f32[128]{0:T(128)}, u32[]{:S(2)}) copy-start(f32[128]{0:T(128)} %param.9) | copy-start | bytes 1540
  8.4 7.8 %copy-start = (f32[128,768]{1,0:T(8,128)S(1)}, f32[128,768]{1,0:T(8,128)}, u32[]{:S(2)}) copy-start(f32[128,768]{1,0:T(8,128)} %param.5) | copy-start | bytes 1179652
  8.5 19.7 %collective-permute-start.1 = (f32[128,768]{1,0:T(8,128)S(1)}, f32[128,768]{1,0:T(8,128)S(1)}, u32[]{:S(2)}, u32[]{:S(2)}) collective-permute-start(f32[128,768]{1,0:T(8,128)S(1)} %broadcast_multiply_fusion), channel_id=1, source_target_pairs={{0,30},{2,0},{4,2},{6,4},{8,6},{10,8},{12,10},{14,12},{16,14},{18,... | collective-permute-start | bytes 1179656 | tf_op jit(solution)/shard_map/ppermute | solution.py:23
  14.0 16.0 %collective-permute-start = (f32[128,768]{1,0:T(8,128)S(1)}, f32[128,768]{1,0:T(8,128)S(1)}, u32[]{:S(2)}, u32[]{:S(2)}) collective-permute-start(f32[128,768]{1,0:T(8,128)S(1)} %broadcast_multiply_fusion), channel_id=1, source_target_pairs={{0,2},{2,4},{4,6},{6,8},{8,10},{10,12},{12,14},{14,16},{16,18},{18... | collective-permute-start | bytes 1179656 | tf_op jit(solution)/shard_map/ppermute | solution.py:23
  14.0 13.2 %collective-permute-start.2 = (f32[128]{0:T(128)S(1)}, f32[128]{0:T(128)S(1)}, u32[]{:S(2)}, u32[]{:S(2)}) collective-permute-start(f32[128]{0:T(128)S(1)} %copy-done.3), channel_id=1, source_target_pairs={{0,1},{1,0},{2,3},{3,2},{4,5},{5,4},{6,7},{7,6},{8,9},{9,8},{10,11... | collective-permute-start | bytes 1544 | tf_op jit(solution)/shard_map/ppermute | solution.py:13
  34.8 11.7 %collective-permute-start.4 = (f32[128,768]{1,0:T(8,128)}, f32[128,768]{1,0:T(8,128)S(1)}, u32[]{:S(2)}, u32[]{:S(2)}) collective-permute-start(f32[128,768]{1,0:T(8,128)} %convolution_multiply_fusion), channel_id=1, source_target_pairs={{0,30},{2,0},{4,2},{6,4},{8,6},{10,8},{12,10},{14,12},{16,14},{18,... | collective-permute-start | bytes 1179656 | tf_op jit(solution)/shard_map/ppermute | solution.py:23
  38.8 9.9 %collective-permute-start.3 = (f32[128,768]{1,0:T(8,128)S(1)}, f32[128,768]{1,0:T(8,128)S(1)}, u32[]{:S(2)}, u32[]{:S(2)}) collective-permute-start(f32[128,768]{1,0:T(8,128)S(1)} %convolution_multiply_fusion.1), channel_id=1, source_target_pairs={{0,2},{2,4},{4,6},{6,8},{8,10},{10,12},{12,14},{14,16},{16,18},{18... | collective-permute-start | bytes 1179656 | tf_op jit(solution)/shard_map/ppermute | solution.py:23
  38.8 0.7 %copy-start.4 = (u32[32]{0:T(128)S(1)}, u32[32]{0:T(128)}, u32[]{:S(2)}) copy-start(u32[32]{0:T(128)} %constant.30) | copy-start | bytes 388
  50.4 1.3 %copy-start.2 = (f32[128,768]{1,0:T(8,128)S(1)}, f32[128,768]{1,0:T(8,128)}, u32[]{:S(2)}) copy-start(f32[128,768]{1,0:T(8,128)} %reduce-scatter.2.cloned.1.call-done) | copy-start | bytes 1179652
Sparse Core Ops, SparseCore 0:
  32.9 17.4 reduce-scatter.1
